TPU v7x, 256 devices: a whole 4x4x8 slice. The times are simulated.
256 devices in a mesh: freq: 8 (over z), lat: 8 (over x, y_hi), lon: 4 (over y_lo, core).
Axes of the slice: x: 4, y: 4 (y_hi: 2, y_lo: 2; y = y_hi * 2 + y_lo), z: 8, core: 2. Of those that a mesh axis runs over, the one named last changes fastest.
Arguments:
- direction: float32 [3, 32, 1024, 2048], P(None, 'freq', 'lat', 'lon'), may hold values from -6 to 6
- base_flow: float32 [2, 32, 1024, 2048], P(None, 'freq', 'lat', 'lon'), may hold values from -2 to 2
- water_depth: float32 [1024, 2048], P('lat', 'lon'), may hold values from 0.5 to 2
- drag_factor: float32 [1024, 2048], P('lat', 'lon'), may hold values from 0.2 to 2
- wet_mask: int32 [1024, 2048], P('lat', 'lon'), may hold values 0 or 1
Outputs:
- result: float32 [3, 32, 1024, 2048], P(None, 'freq', 'lat', 'lon')
All inputs are finite; a program needn't handle non-finite values. No bound on the sum of `wet_mask` on one device may be relied on, other than what follows from the above.
Results may differ from a plain program's by a relative error of at most 0.000071.
Values sent between devices are 32-bit elements; how exact they have to be, the bound alone decides.
A program may use at most 128 MiB of HBM per device.

v0:
```python
import math
import jax
import jax.numpy as jnp
from jax import lax
from jax.sharding import PartitionSpec as P

NCON = 16
NTIME = 256
LINEAR_DRAG = 0.5
GRAVITY = 1.0
OMEGA_STEP = 0.25
SPEED_SOFT = 0.01


def extended_2(block, sides, width):
    for axis, dim in sides:
        count = lax.axis_size(axis)
        forward = [(i, i + 1) for i in range(count - 1)]
        forward.append((count - 1, 0))
        backward = [(target, source) for source, target in forward]
        low = lax.ppermute(
            lax.slice_in_dim(block, block.shape[dim] - width, None, axis=dim), axis, forward
        )
        high = lax.ppermute(lax.slice_in_dim(block, 0, width, axis=dim), axis, backward)
        block = jnp.concatenate([low, block, high], axis=dim)
    return block


def samples_table(sample_count, constituents):
    sample_index = jnp.arange(sample_count, dtype=jnp.int32)
    harmonic = jnp.arange(1, constituents + 1, dtype=jnp.int32)
    wrapped_turns = sample_index[:, None] * harmonic[None, :] % sample_count
    phase_angle = wrapped_turns.astype(jnp.float32) * (2.0 * math.pi / sample_count)
    table = jnp.stack([jnp.cos(phase_angle), jnp.sin(phase_angle)], axis=2)
    return table.reshape(sample_count, 2 * constituents)


def rotation_of(row_index, total_rows):
    return 0.5 + (row_index.astype(jnp.float32) + 0.5) / total_rows


def tendency(values, angular):
    cos_sin = values.reshape((values.shape[0] // 2, 2) + values.shape[1:])
    moved = jnp.stack([angular * cos_sin[:, 1], -angular * cos_sin[:, 0]], axis=1)
    return moved.reshape(values.shape)


def linear_residual(extended, tile_rows, tile_cols, angular, rotation):

    def neighbour(plane, row_step, col_step):
        return extended[
            plane,
            :,
            1 + row_step : 1 + row_step + tile_rows,
            1 + col_step : 1 + col_step + tile_cols,
        ]

    height = neighbour(0, 0, 0)
    east = neighbour(1, 0, 0)
    north = neighbour(2, 0, 0)
    res_height = (
        tendency(height, angular)
        + neighbour(3, 0, 0)
        - neighbour(3, 0, -1)
        + neighbour(4, 0, 0)
        - neighbour(4, -1, 0)
    )
    north_mean = 0.25 * (north + neighbour(2, 0, 1) + neighbour(2, -1, 0) + neighbour(2, -1, 1))
    east_mean = 0.25 * (east + neighbour(1, 0, -1) + neighbour(1, 1, 0) + neighbour(1, 1, -1))
    res_east = (
        tendency(east, angular)
        + LINEAR_DRAG * east
        - rotation * north_mean
        + GRAVITY * (neighbour(0, 0, 1) - height)
    )
    res_north = (
        tendency(north, angular)
        + LINEAR_DRAG * north
        + rotation * east_mean
        + GRAVITY * (neighbour(0, 1, 0) - height)
    )
    return jnp.stack([res_height, res_east, res_north])


def friction_row(row_block, drag_row, table):
    highest = lax.Precision.HIGHEST
    series = jnp.einsum("tc,fcn->ftn", table, row_block, precision=highest)
    base_east, base_north, step_east, step_north = (series[0], series[1], series[2], series[3])
    magnitude = jnp.sqrt(base_east * base_east + base_north * base_north + SPEED_SOFT)
    projected = (base_east * step_east + base_north * step_north) / magnitude
    force_east = drag_row * (magnitude * step_east + base_east * projected)
    force_north = drag_row * (magnitude * step_north + base_north * projected)
    forces = jnp.stack([force_east, force_north])
    analysed = jnp.einsum("tc,ftn->fcn", table, forces, precision=highest) * (2.0 / table.shape[0])
    drag_rate = drag_row * jnp.mean(magnitude, axis=0)
    return (analysed, drag_rate)


def precondition(residual, angular, rotation, drag_rate):
    shaped = residual.reshape((3, residual.shape[1] // 2, 2) + residual.shape[2:])
    cos_part = shaped[:, :, 0]
    sin_part = shaped[:, :, 1]
    height_cos = -sin_part[0] / angular
    height_sin = cos_part[0] / angular
    real_rate = drag_rate + LINEAR_DRAG
    det_real = real_rate * real_rate - angular * angular + rotation * rotation
    det_imag = 2.0 * real_rate * angular
    det_norm = det_real * det_real + det_imag * det_imag
    inv_real = det_real / det_norm
    inv_imag = -det_imag / det_norm
    east_re = cos_part[1]
    east_im = -sin_part[1]
    north_re = cos_part[2]
    north_im = -sin_part[2]
    num_east_re = real_rate * east_re - angular * east_im + rotation * north_re
    num_east_im = real_rate * east_im + angular * east_re + rotation * north_im
    num_north_re = -rotation * east_re + real_rate * north_re - angular * north_im
    num_north_im = -rotation * east_im + real_rate * north_im + angular * north_re
    east_out_re = num_east_re * inv_real - num_east_im * inv_imag
    east_out_im = num_east_re * inv_imag + num_east_im * inv_real
    north_out_re = num_north_re * inv_real - num_north_im * inv_imag
    north_out_im = num_north_re * inv_imag + num_north_im * inv_real
    cosines = jnp.stack([height_cos, east_out_re, north_out_re])
    sines = jnp.stack([height_sin, -east_out_im, -north_out_im])
    return jnp.stack([cosines, sines], axis=2).reshape(residual.shape)


def friction_band(flows_band, drag_band, table):
    highest = lax.Precision.HIGHEST
    fields, coefs, rows, cols = flows_band.shape
    block = flows_band.reshape(fields, coefs, rows * cols)
    series = jnp.einsum("tc,fcn->ftn", table, block, precision=highest)
    base_east, base_north, step_east, step_north = (series[0], series[1], series[2], series[3])
    drag_row = drag_band.reshape(1, rows * cols)
    magnitude = jnp.sqrt(base_east * base_east + base_north * base_north + SPEED_SOFT)
    projected = (base_east * step_east + base_north * step_north) / magnitude
    force_east = drag_row * (magnitude * step_east + base_east * projected)
    force_north = drag_row * (magnitude * step_north + base_north * projected)
    forces = jnp.stack([force_east, force_north])
    analysed = jnp.einsum("tc,ftn->fcn", table, forces, precision=highest) * (2.0 / table.shape[0])
    drag_rate = drag_row[0] * lax.optimization_barrier(jnp.mean(magnitude, axis=0))
    return (analysed.reshape(2, coefs, rows, cols), drag_rate.reshape(rows, cols))


def local(direction, base_flow, water_depth, drag_factor, wet_mask):
    local_coefs = direction.shape[1]
    tile_rows = direction.shape[2]
    tile_cols = direction.shape[3]
    groups = lax.axis_size("freq")
    member = lax.axis_index("freq")
    band_rows = tile_rows // groups
    lat_place = lax.axis_index("lat")
    lat_count = lax.axis_size("lat")
    total_rows = tile_rows * lat_count
    wet_cells = wet_mask.astype(jnp.float32)
    height = direction[0] * wet_cells
    east = direction[1] * wet_cells
    north = direction[2] * wet_cells
    flows = jnp.concatenate([base_flow, jnp.stack([east, north])], axis=0)
    flows_band = lax.all_to_all(flows, "freq", split_axis=2, concat_axis=1, tiled=True)
    planes = jnp.stack([height, east, north, water_depth * east, water_depth * north])
    extended = extended_2(planes, (("lat", 2), ("lon", 3)), 1)
    rim_keep = jnp.ones((tile_rows + 2,), jnp.float32)
    rim_keep = rim_keep.at[0].set(jnp.where(lat_place == 0, 0.0, 1.0))
    rim_keep = rim_keep.at[tile_rows + 1].set(jnp.where(lat_place == lat_count - 1, 0.0, 1.0))
    extended = extended * rim_keep[:, None]
    local_count = local_coefs // 2
    first_con = member * local_count
    angular_local = OMEGA_STEP * (first_con + jnp.arange(local_count, dtype=jnp.int32) + 1).astype(
        jnp.float32
    )
    row_global = lat_place * tile_rows + jnp.arange(tile_rows, dtype=jnp.int32)
    rotation = rotation_of(row_global, total_rows)
    linear_part = linear_residual(
        extended, tile_rows, tile_cols, angular_local[:, None, None], rotation[:, None]
    )
    table = samples_table(NTIME, NCON)
    band_start = member * band_rows
    drag_band = lax.dynamic_slice_in_dim(drag_factor, band_start, band_rows, 0)
    analysed_band, drag_rate_band = friction_band(flows_band, drag_band, table)
    friction = lax.all_to_all(analysed_band, "freq", split_axis=1, concat_axis=2, tiled=True)
    drag_rate = lax.all_gather(drag_rate_band, "freq", axis=0, tiled=True)
    residual = (
        linear_part + jnp.concatenate([jnp.zeros_like(friction[:1]), friction], axis=0)
    ) * wet_cells
    return precondition(residual, angular_local[:, None, None], rotation[:, None], drag_rate)


def solution(mesh):
    placed = (
        P(None, "freq", "lat", "lon"),
        P(None, "freq", "lat", "lon"),
        P("lat", "lon"),
        P("lat", "lon"),
        P("lat", "lon"),
    )
    return jax.shard_map(
        local, mesh=mesh, in_specs=placed, out_specs=P(None, "freq", "lat", "lon"), check_vma=False
    )
```

profile of v0, /device:TPU:2, one launch (start us, length us, event | category | flops | bytes accessed | tf_op | source)
XLA Modules:
  0.0 294.2 jit_solution(5827438192637905519)
XLA Ops:
  0.0 0.0 copy-start
  0.0 1.0 convert_element_type.48
  1.0 2.4 multiply_dynamic-update-slice_fusion.2
  3.4 2.5 constant_dynamic-update-slice_fusion.1
  5.9 2.7 constant_dynamic-update-slice_fusion
  8.5 0.7 copy.89
  9.2 0.7 copy.88
  9.9 0.0 copy-done.4
  9.9 1.4 copy.87
  11.3 2.7 pad_maximum_fusion
  13.9 9.2 %all-to-all-start = ((f32[4,4,128,512]{3,1,0,2:T(4,128)}), f32[4,4,128,512]{3,1,0,2:T(4,128)}, u32[]{:S(2)}, u32[]{:S(2)}) async-start(f32[4,4,128,512]{3,1,0,2:T(4,128)} %pad_maximum_fusion), calls=%async_computation | async-start | bytes 8388608 | tf_op jit(solution)/shard_map/all_to_all | solution.py:160
  23.1 0.2 fusion.33
  23.4 0.0 copy-done
  23.4 0.0 copy-done.5
  23.4 1.2 multiply_dynamic-update-slice_fusion.1
  24.6 1.2 multiply_dynamic-update-slice_fusion
  25.8 93.7 %all-to-all-done = f32[4,4,128,512]{3,1,0,2:T(4,128)} async-done(((f32[4,4,128,512]{3,1,0,2:T(4,128)}), f32[4,4,128,512]{3,1,0,2:T(4,128)}, u32[]{:S(2)}, u32[]{:S(2)}) %all-to-all-start) | async-done | bytes 4194336 | tf_op jit(solution)/shard_map/all_to_all | solution.py:160
  119.4 6.6 %copy.110 = f32[4,4,8,16,512]{4,3,1,2,0:T(8,128)} copy(f32[4,4,8,16,512]{4,1,0,3,2:T(4,128)} %bitcast.8) | data formatting | bytes 8388608 | tf_op jit(solution)/shard_map/all_to_all | solution.py:160
  126.1 5.0 %reshape.520 = f32[4,32,8192]{2,1,0:T(8,128)} reshape(f32[4,8,4,16,512]{4,3,2,1,0:T(8,128)} %bitcast.142) | data formatting | bytes 8388608 | tf_op jit(solution)/shard_map/reshape | solution.py:131
  131.1 47.7 %convolution_bitcast_fusion = f32[4,256,8192]{2,1,0:T(8,128)} fusion(f32[4,32,8192]{2,1,0:T(8,128)} %reshape.520, f32[256,32,1]{0,1,2:T(8,128)S(1)} %reshape.526), kind=kOutput, calls=%fused_computation | convolution fusion | flops 3221225472 | bytes 37781504 | tf_op jit(solution)/shard_map/tc,fcn->ftn/dot_general | solution.py:132
  178.8 18.2 %add_multiply_fusion.1 = (f32[1,256,8192]{2,1,0:T(8,128)}, f32[1,256,8192]{2,1,0:T(8,128)}, f32[8192]{0:T(1024)S(1)}) fusion(f32[4,256,8192]{2,1,0:T(8,128)} %convolution_bitcast_fusion, f32[8192]{0:T(1024)S(1)} %bitcast.154), kind=kLoop, calls=%fused_computation.7 | loop fusion | flops 35643392 | bytes 50397184 | tf_op jit(solution)/shard_map/mul | solution.py:137
  197.0 13.7 %fusion.4 = f32[2,8192,32]{1,2,0:T(8,128)S(1)} fusion(f32[256,32,1]{0,1,2:T(8,128)S(1)} %reshape.526, f32[1,256,8192]{2,1,0:T(8,128)} %get-tuple-element.40, f32[1,256,8192]{2,1,0:T(8,128)} %get-tuple-element.39), kind=kOutput, calls=%fused_computation.5 | convolution fusion | flops 1615331328 | bytes 18907136 | tf_op jit(solution)/shard_map/tc,ftn->fcn/dot_general | solution.py:140
  210.7 1.2 copy.108
  211.9 1.6 copy.92
  213.5 3.6 %all-to-all-start.1 = ((f32[2,32,16,512]{3,2,0,1:T(8,128)}), f32[2,32,16,512]{3,2,0,1:T(8,128)S(1)}, u32[]{:S(2)}, u32[]{:S(2)}) async-start(f32[2,32,16,512]{3,2,0,1:T(8,128)} %copy.92), calls=%async_computation.1 | async-start | bytes 4194304 | tf_op jit(solution)/shard_map/all_to_all | solution.py:181
  217.1 1.1 fusion.40
  218.3 3.3 %collective-permute-start = (f32[5,4,1,512]{3,2,1,0:T(1,128)S(1)}, f32[5,4,1,512]{3,2,1,0:T(1,128)S(1)}, u32[]{:S(2)}, u32[]{:S(2)}) collective-permute-start(f32[5,4,1,512]{3,2,1,0:T(1,128)S(1)} %get-tuple-element.49), channel_id=1, source_target_pairs={{0,4},{4,8},{8,12},{12,16},{16,20},{20,24},{24,28},{28,0},{1,5},{5... | collective-permute-start | bytes 122888 | tf_op jit(solution)/shard_map/ppermute | solution.py:21
  221.5 1.4 collective-permute-start.1
  223.0 1.7 collective-permute-done
  224.7 2.5 collective-permute-done.1
  227.2 3.8 %pad_maximum_fusion.4 = (f32[5,4,130,1]{3,2,1,0:T(8,128)}, f32[5,4,130,1]{3,2,1,0:T(8,128)}) fusion(f32[5,4,1,512]{3,2,1,0:T(1,128)S(1)} %collective-permute-done.1, f32[5,4,128,512]{3,2,1,0:T(8,128)} %multiply_dynamic-update-slice_fusion, f32[5,4,1,512]{3,2,1,0:T(1,128)S(1)} %collective-permute-done), kind=kLoop, calls=%fused_computation.22 | loop fusion | flops 10400 | bytes 5345600 | tf_op jit(solution)/shard_map/slice | solution.py:22
  231.0 2.5 copy.83
  233.5 0.1 collective-permute-start.2
  233.6 2.6 copy.84
  236.2 1.8 collective-permute-start.3
  238.0 0.0 collective-permute-done.2
  238.0 1.6 copy.85
  239.6 0.0 collective-permute-done.3
  239.6 1.6 copy.86
  241.2 6.2 %maximum_multiply_fusion = f32[5,4,130,514]{3,2,1,0:T(8,128)S(1)} fusion(f32[5,4,130,1]{3,2,1,0:T(8,128)} %copy.86, f32[5,4,1,512]{3,2,1,0:T(1,128)S(1)} %collective-permute-done.1, f32[5,4,128,512]{3,2,1,0:T(8,128)} %multiply_dynamic-update-slice_fusion, f32[5,4,1,512]{3,2,1,0:T(1,128)S(1)} %collective-permute-done, f32[5,4,130,1]{3,2,1,0:T(8,128)} %copy.85, ...), kind=kLoop, calls=%fused_computation.12 | loop fusion | flops 6682000 | bytes 10691720 | tf_op jit(solution)/shard_map/mul | solution.py:166
  247.5 0.4 slice.187
  247.8 0.2 slice_multiply_fusion.8
  248.1 0.1 pad_maximum_fusion.5
  248.1 2.7 slice_subtract_fusion.2
  250.8 0.4 slice_multiply_fusion.4
  251.2 0.1 pad_maximum_fusion.7
  251.3 0.1 pad_maximum_fusion.6
  251.4 3.9 %fusion.12 = (f32[1,4,128,512]{3,2,1,0:T(8,128)}, f32[1,4,128,512]{3,2,1,0:T(8,128)}) fusion(f32[5,4,130,514]{3,2,1,0:T(8,128)S(1)} %maximum_multiply_fusion, f32[128]{0:T(128)S(1)} %broadcast_multiply_fusion.2, f32[1,4,128,512]{3,2,1,0:T(8,128)S(1)} %bitcast.151, f32[1,4,128,512]{3,2,1,0:T(8,128)S(1)} %bitcast.150), kind=kLoop, calls=%fused_computation.31 | loop fusion | flops 4718592 | bytes 15729152 | tf_op jit(solution)/shard_map/add | solution.py:71
  255.3 31.2 %all_gather.3 = f32[128,512]{1,0:T(8,128)S(1)} all-gather(f32[16,512]{1,0:T(8,128)S(1)} %reshape.524), channel_id=1, replica_groups=mesh['freq'=8,'lat'=8,'lon'=4] {'freq'}, dimensions={0}, use_global_device_ids=true | all-gather | bytes 294912 | tf_op jit(solution)/shard_map/all_gather | solution.py:182
  286.6 0.1 broadcast_add_fusion
  286.6 0.0 all-to-all-done.1
  286.6 0.0 copy-start.2
  286.7 0.0 copy-start.3
  286.7 0.2 copy.94
  286.8 1.0 copy-done.2
  287.9 0.3 copy-done.3
  288.2 1.9 fusion.8
  290.1 0.8 multiply_subtract_fusion.2
  290.9 0.1 maximum_bitcast_fusion
  291.0 0.4 add_negate_fusion.1
  291.4 0.1 maximum_bitcast_fusion.1
  291.6 0.0 copy-start.1
  291.6 0.3 pad_maximum_fusion.1
  291.9 2.0 copy.100
  (19 shorter events, 0.2 us)
Async XLA Ops:
  0.0 23.4 %copy-start = (f32[128,512]{1,0:T(8,128)S(1)}, f32[128,512]{1,0:T(8,128)}, u32[]{:S(2)}) copy-start(f32[128,512]{1,0:T(8,128)} %param.12) | copy-start | bytes 786436
  5.9 4.0 %copy-start.4 = (f32[2,4,128,512]{3,2,1,0:T(8,128)S(1)}, f32[2,4,128,512]{3,2,1,0:T(8,128)}, u32[]{:S(2)}) copy-start(f32[2,4,128,512]{3,2,1,0:T(8,128)} %param.10) | copy-start | bytes 6291460
  13.9 9.5 %copy-start.5 = (f32[128,512]{1,0:T(8,128)S(1)}, f32[128,512]{1,0:T(8,128)}, u32[]{:S(2)}) copy-start(f32[128,512]{1,0:T(8,128)} %param.11) | copy-start | bytes 786436
  13.9 105.5 %all-to-all-start = ((f32[4,4,128,512]{3,1,0,2:T(4,128)}), f32[4,4,128,512]{3,1,0,2:T(4,128)}, u32[]{:S(2)}, u32[]{:S(2)}) async-start(f32[4,4,128,512]{3,1,0,2:T(4,128)} %pad_maximum_fusion), calls=%async_computation | async-start | bytes 8388608 | tf_op jit(solution)/shard_map/all_to_all | solution.py:160
  213.5 73.1 %all-to-all-start.1 = ((f32[2,32,16,512]{3,2,0,1:T(8,128)}), f32[2,32,16,512]{3,2,0,1:T(8,128)S(1)}, u32[]{:S(2)}, u32[]{:S(2)}) async-start(f32[2,32,16,512]{3,2,0,1:T(8,128)} %copy.92), calls=%async_computation.1 | async-start | bytes 4194304 | tf_op jit(solution)/shard_map/all_to_all | solution.py:181
  218.3 6.5 %collective-permute-start = (f32[5,4,1,512]{3,2,1,0:T(1,128)S(1)}, f32[5,4,1,512]{3,2,1,0:T(1,128)S(1)}, u32[]{:S(2)}, u32[]{:S(2)}) collective-permute-start(f32[5,4,1,512]{3,2,1,0:T(1,128)S(1)} %get-tuple-element.49), channel_id=1, source_target_pairs={{0,4},{4,8},{8,12},{12,16},{16,20},{20,24},{24,28},{28,0},{1,5},{5... | collective-permute-start | bytes 122888 | tf_op jit(solution)/shard_map/ppermute | solution.py:21
  221.5 5.7 %collective-permute-start.1 = (f32[5,4,1,512]{3,2,1,0:T(1,128)S(1)}, f32[5,4,1,512]{3,2,1,0:T(1,128)S(1)}, u32[]{:S(2)}, u32[]{:S(2)}) collective-permute-start(f32[5,4,1,512]{3,2,1,0:T(1,128)S(1)} %get-tuple-element.50), channel_id=1, source_target_pairs={{4,0},{8,4},{12,8},{16,12},{20,16},{24,20},{28,24},{0,28},{5,1},{9... | collective-permute-start | bytes 122888 | tf_op jit(solution)/shard_map/ppermute | solution.py:24
  233.5 4.4 %collective-permute-start.2 = (f32[5,4,130,1]{2,0,3,1:T(8,128)S(1)}, f32[5,4,130,1]{2,0,3,1:T(8,128)S(1)}, u32[]{:S(2)}, u32[]{:S(2)}) collective-permute-start(f32[5,4,130,1]{2,0,3,1:T(8,128)S(1)} %copy.83), channel_id=1, source_target_pairs={{0,1},{1,2},{2,3},{3,0},{4,5},{5,6},{6,7},{7,4},{8,9},{9,10},{10,1... | collective-permute-start | bytes 31208 | tf_op jit(solution)/shard_map/ppermute | solution.py:21
  236.2 3.4 %collective-permute-start.3 = (f32[5,4,130,1]{2,0,3,1:T(8,128)S(1)}, f32[5,4,130,1]{2,0,3,1:T(8,128)S(1)}, u32[]{:S(2)}, u32[]{:S(2)}) collective-permute-start(f32[5,4,130,1]{2,0,3,1:T(8,128)S(1)} %copy.84), channel_id=1, source_target_pairs={{1,0},{2,1},{3,2},{0,3},{5,4},{6,5},{7,6},{4,7},{9,8},{10,9},{11,1... | collective-permute-start | bytes 31208 | tf_op jit(solution)/shard_map/ppermute | solution.py:24
  286.6 1.2 copy-start.2
  286.7 1.5 copy-start.3
  291.6 2.3 copy-start.1
where the time goes:
time: 298 us; the launch traced here: 294 us
  waiting for transfers between devices  97.9 us (33%)
  matrix products  61.4 us (21%)
  other arithmetic  53.1 us (18%)
  blocking collectives  31.2 us (10%)
  local copies, waits for them, and re-layouts  30.6 us (10%)
  starting transfers between devices  19.3 us (6%)
    all_to_all x1, waiting for transfers between devices, local(): lax.all_to_all(flows, 'freq', split_axis=2, concat_axis=1, tiled=True)  93.7 us
    dot_general x1, matrix products, friction_band(): series = jnp.einsum('tc,fcn->ftn', table, block, precision=highest)  47.7 us
    all_gather x1, blocking collectives, local(): drag_rate = lax.all_gather(drag_rate_band, 'freq', axis=0, tiled=True)  31.2 us
    mul x1, other arithmetic, friction_band(): force_east = drag_row * (magnitude * step_east + base_east * projected)  18.2 us
    dot_general x1, matrix products, friction_band(): jnp.einsum('tc,ftn->fcn', table, forces, precision=highest)  13.7 us
    all_to_all x1, starting transfers between devices, local(): lax.all_to_all(flows, 'freq', split_axis=2, concat_axis=1, tiled=True)  9.18 us
    unnamed x4, other arithmetic  8.68 us
    all_to_all x1, local copies, waits for them, and re-layouts, local(): lax.all_to_all(flows, 'freq', split_axis=2, concat_axis=1, tiled=True)  6.64 us
  transfers between devices with their start and end apart: 6, of which 3 were waited for; matrix products, arithmetic and copies ran while one was open for 10% of the time, Pallas kernels for 0%

commit v1 on v0

--- a/solution.py
+++ b/solution.py
@@ -179,7 +179,9 @@
     drag_band = lax.dynamic_slice_in_dim(drag_factor, band_start, band_rows, 0)
     analysed_band, drag_rate_band = friction_band(flows_band, drag_band, table)
     friction = lax.all_to_all(analysed_band, "freq", split_axis=1, concat_axis=2, tiled=True)
-    drag_rate = lax.all_gather(drag_rate_band, "freq", axis=0, tiled=True)
+    drag_rate = jnp.concatenate(
+        lax.all_to_all(jnp.stack([drag_rate_band] * lax.axis_size("freq")), "freq", 0, 0), axis=0
+    )
     residual = (
         linear_part + jnp.concatenate([jnp.zeros_like(friction[:1]), friction], axis=0)
     ) * wet_cells

time: 298 us -> 287 us (0.963)
  blocking collectives: 31.2 us -> 0 us
  waiting for transfers between devices: 97.9 us -> 111 us
  starting transfers between devices: 19.3 us -> 26.2 us
    all_gather x1 -> x0, blocking collectives: 31.2 us -> none  [local(): drag_rate = lax.all_gather(drag_rate_band, 'freq', axis=0, tiled=True)]
    all_to_all x1, waiting for transfers between devices: 0.01 us -> 12.8 us  [local(): lax.all_to_all(analysed_band, 'freq', split_axis=1, concat_axis=2, tiled=...]
    all_to_all x1, starting transfers between devices: 3.6 us -> 7.12 us  [local(): lax.all_to_all(analysed_band, 'freq', split_axis=1, concat_axis=2, tiled=...]
    all_to_all x0 -> x1, starting transfers between devices: none -> 3.41 us  [local(): lax.all_to_all(jnp.stack([drag_rate_band] * lax.axis_size('freq')), 'freq...]
  transfers between devices with their start and end apart: 6 -> 7, of which waited for: 3 -> 4; matrix products, arithmetic and copies ran while one was open for 10% -> 16% of each run, Pallas kernels for 0% -> 0%
where the time goes in v1:
time: 287 us; the launch traced here: 283 us
  waiting for transfers between devices  111 us (39%)
  matrix products  61.4 us (21%)
  other arithmetic  53 us (18%)
  local copies, waits for them, and re-layouts  31.3 us (11%)
  starting transfers between devices  26.2 us (9%)
    all_to_all x1, waiting for transfers between devices, local(): lax.all_to_all(flows, 'freq', split_axis=2, concat_axis=1, tiled=True)  93.7 us
    dot_general x1, matrix products, friction_band(): series = jnp.einsum('tc,fcn->ftn', table, block, precision=highest)  47.7 us
    mul x1, other arithmetic, friction_band(): force_east = drag_row * (magnitude * step_east + base_east * projected)  18.2 us
    dot_general x1, matrix products, friction_band(): jnp.einsum('tc,ftn->fcn', table, forces, precision=highest)  13.7 us
    all_to_all x1, waiting for transfers between devices, local(): lax.all_to_all(analysed_band, 'freq', split_axis=1, concat_axis=2, tiled=...  12.8 us
    all_to_all x1, starting transfers between devices, local(): lax.all_to_all(flows, 'freq', split_axis=2, concat_axis=1, tiled=True)  9.12 us
    unnamed x4, other arithmetic  8.66 us
    all_to_all x1, starting transfers between devices, local(): lax.all_to_all(analysed_band, 'freq', split_axis=1, concat_axis=2, tiled=...  7.12 us
  transfers between devices with their start and end apart: 7, of which 4 were waited for; matrix products, arithmetic and copies ran while one was open for 16% of the time, Pallas kernels for 0%

profile of v1, /device:TPU:2, one launch (start us, length us, event | category | flops | bytes accessed | tf_op | source)
XLA Modules:
  0.0 283.3 jit_solution(1385850749049875702)
XLA Ops:
  0.0 0.0 copy-start
  0.0 1.0 convert_element_type.48
  1.0 2.3 multiply_dynamic-update-slice_fusion.2
  3.4 2.5 constant_dynamic-update-slice_fusion.1
  5.9 2.6 constant_dynamic-update-slice_fusion
  8.5 0.7 copy.89
  9.2 0.7 copy.88
  9.9 0.0 copy-done.4
  9.9 1.4 copy.87
  11.3 2.7 pad_maximum_fusion
  13.9 9.1 %all-to-all-start = ((f32[4,4,128,512]{3,1,0,2:T(4,128)}), f32[4,4,128,512]{3,1,0,2:T(4,128)}, u32[]{:S(2)}, u32[]{:S(2)}) async-start(f32[4,4,128,512]{3,1,0,2:T(4,128)} %pad_maximum_fusion), calls=%async_computation | async-start | bytes 8388608 | tf_op jit(solution)/shard_map/all_to_all | solution.py:160
  23.1 0.2 fusion.33
  23.3 0.0 copy-done
  23.3 0.0 copy-done.5
  23.4 1.2 multiply_dynamic-update-slice_fusion.1
  24.5 1.2 multiply_dynamic-update-slice_fusion
  25.7 93.7 %all-to-all-done = f32[4,4,128,512]{3,1,0,2:T(4,128)} async-done(((f32[4,4,128,512]{3,1,0,2:T(4,128)}), f32[4,4,128,512]{3,1,0,2:T(4,128)}, u32[]{:S(2)}, u32[]{:S(2)}) %all-to-all-start) | async-done | bytes 4194336 | tf_op jit(solution)/shard_map/all_to_all | solution.py:160
  119.4 6.6 %copy.110 = f32[4,4,8,16,512]{4,3,1,2,0:T(8,128)} copy(f32[4,4,8,16,512]{4,1,0,3,2:T(4,128)} %bitcast.8) | data formatting | bytes 8388608 | tf_op jit(solution)/shard_map/all_to_all | solution.py:160
  126.0 5.0 %reshape.532 = f32[4,32,8192]{2,1,0:T(8,128)} reshape(f32[4,8,4,16,512]{4,3,2,1,0:T(8,128)} %bitcast.145) | data formatting | bytes 8388608 | tf_op jit(solution)/shard_map/reshape | solution.py:131
  131.0 47.7 %convolution_bitcast_fusion = f32[4,256,8192]{2,1,0:T(8,128)} fusion(f32[4,32,8192]{2,1,0:T(8,128)} %reshape.532, f32[256,32,1]{0,1,2:T(8,128)S(1)} %reshape.537), kind=kOutput, calls=%fused_computation | convolution fusion | flops 3221225472 | bytes 37781504 | tf_op jit(solution)/shard_map/tc,fcn->ftn/dot_general | solution.py:132
  178.7 18.2 %add_multiply_fusion.1 = (f32[1,256,8192]{2,1,0:T(8,128)}, f32[1,256,8192]{2,1,0:T(8,128)}, f32[8192]{0:T(1024)S(1)}) fusion(f32[4,256,8192]{2,1,0:T(8,128)} %convolution_bitcast_fusion, f32[8192]{0:T(1024)S(1)} %bitcast.158), kind=kLoop, calls=%fused_computation.7 | loop fusion | flops 35643392 | bytes 50397184 | tf_op jit(solution)/shard_map/mul | solution.py:137
  196.9 0.7 stack.33
  197.7 3.4 %all-to-all-start.2 = ((f32[8,16,512]{2,1,0:T(8,128)}), f32[8,16,512]{2,1,0:T(8,128)S(1)}, u32[]{:S(2)}, u32[]{:S(2)}) async-start(f32[8,16,512]{2,1,0:T(8,128)} %stack.33), calls=%async_computation.2 | async-start | bytes 524288 | tf_op jit(solution)/shard_map/all_to_all | solution.py:183
  201.1 13.7 %fusion.4 = f32[2,8192,32]{1,2,0:T(8,128)S(1)} fusion(f32[256,32,1]{0,1,2:T(8,128)S(1)} %reshape.537, f32[1,256,8192]{2,1,0:T(8,128)} %get-tuple-element.40, f32[1,256,8192]{2,1,0:T(8,128)} %get-tuple-element.39), kind=kOutput, calls=%fused_computation.5 | convolution fusion | flops 1615331328 | bytes 18907136 | tf_op jit(solution)/shard_map/tc,ftn->fcn/dot_general | solution.py:140
  214.8 1.2 copy.108
  216.0 1.6 copy.92
  217.6 0.0 all-to-all-done.2
  217.6 7.1 %all-to-all-start.1 = ((f32[2,32,16,512]{3,2,0,1:T(8,128)}), f32[2,32,16,512]{3,2,0,1:T(8,128)S(1)}, u32[]{:S(2)}, u32[]{:S(2)}) async-start(f32[2,32,16,512]{3,2,0,1:T(8,128)} %copy.92), calls=%async_computation.1 | async-start | bytes 4194304 | tf_op jit(solution)/shard_map/all_to_all | solution.py:181
  224.7 1.1 fusion.39
  225.9 3.3 %collective-permute-start = (f32[5,4,1,512]{3,2,1,0:T(1,128)S(1)}, f32[5,4,1,512]{3,2,1,0:T(1,128)S(1)}, u32[]{:S(2)}, u32[]{:S(2)}) collective-permute-start(f32[5,4,1,512]{3,2,1,0:T(1,128)S(1)} %get-tuple-element.49), channel_id=1, source_target_pairs={{0,4},{4,8},{8,12},{12,16},{16,20},{20,24},{24,28},{28,0},{1,5},{5... | collective-permute-start | bytes 122888 | tf_op jit(solution)/shard_map/ppermute | solution.py:21
  229.1 1.4 collective-permute-start.1
  230.6 1.7 collective-permute-done
  232.3 2.5 collective-permute-done.1
  234.8 3.8 %pad_maximum_fusion.4 = (f32[5,4,130,1]{3,2,1,0:T(8,128)}, f32[5,4,130,1]{3,2,1,0:T(8,128)}) fusion(f32[5,4,1,512]{3,2,1,0:T(1,128)S(1)} %collective-permute-done.1, f32[5,4,128,512]{3,2,1,0:T(8,128)} %multiply_dynamic-update-slice_fusion, f32[5,4,1,512]{3,2,1,0:T(1,128)S(1)} %collective-permute-done), kind=kLoop, calls=%fused_computation.22 | loop fusion | flops 10400 | bytes 5345600 | tf_op jit(solution)/shard_map/slice | solution.py:22
  238.6 2.5 copy.83
  241.2 0.1 collective-permute-start.2
  241.2 2.6 copy.84
  243.8 1.8 collective-permute-start.3
  245.6 0.0 collective-permute-done.2
  245.6 1.6 copy.85
  247.2 0.0 collective-permute-done.3
  247.2 1.6 copy.86
  248.8 6.2 %maximum_multiply_fusion = f32[5,4,130,514]{3,2,1,0:T(8,128)S(1)} fusion(f32[5,4,130,1]{3,2,1,0:T(8,128)} %copy.86, f32[5,4,1,512]{3,2,1,0:T(1,128)S(1)} %collective-permute-done.1, f32[5,4,128,512]{3,2,1,0:T(8,128)} %multiply_dynamic-update-slice_fusion, f32[5,4,1,512]{3,2,1,0:T(1,128)S(1)} %collective-permute-done, f32[5,4,130,1]{3,2,1,0:T(8,128)} %copy.85, ...), kind=kLoop, calls=%fused_computation.12 | loop fusion | flops 6682000 | bytes 10691720 | tf_op jit(solution)/shard_map/mul | solution.py:166
  255.1 0.4 slice.187
  255.5 0.2 slice_multiply_fusion.8
  255.7 0.1 pad_maximum_fusion.5
  255.8 2.7 slice_subtract_fusion.2
  258.4 0.4 slice_multiply_fusion.4
  258.8 0.1 pad_maximum_fusion.7
  258.9 0.1 pad_maximum_fusion.6
  259.0 3.9 %fusion.12 = (f32[1,4,128,512]{3,2,1,0:T(8,128)}, f32[1,4,128,512]{3,2,1,0:T(8,128)}) fusion(f32[5,4,130,514]{3,2,1,0:T(8,128)S(1)} %maximum_multiply_fusion, f32[128]{0:T(128)S(1)} %broadcast_multiply_fusion.2, f32[1,4,128,512]{3,2,1,0:T(8,128)S(1)} %bitcast.154, f32[1,4,128,512]{3,2,1,0:T(8,128)S(1)} %bitcast.153), kind=kLoop, calls=%fused_computation.31 | loop fusion | flops 4718592 | bytes 15729152 | tf_op jit(solution)/shard_map/add | solution.py:71
  263.0 12.8 %all-to-all-done.1 = f32[2,32,16,512]{3,2,0,1:T(8,128)S(1)} async-done(((f32[2,32,16,512]{3,2,0,1:T(8,128)}), f32[2,32,16,512]{3,2,0,1:T(8,128)S(1)}, u32[]{:S(2)}, u32[]{:S(2)}) %all-to-all-start.1) | async-done | bytes 2097184 | tf_op jit(solution)/shard_map/all_to_all | solution.py:181
  275.8 0.2 copy.94
  276.0 1.0 copy-done.2
  277.0 0.3 copy-done.3
  277.4 1.9 fusion.8
  279.3 0.8 multiply_subtract_fusion.2
  280.1 0.1 maximum_bitcast_fusion
  280.2 0.4 add_negate_fusion.1
  280.6 0.1 maximum_bitcast_fusion.1
  280.8 0.0 copy-start.1
  280.8 0.3 pad_maximum_fusion.1
  281.1 2.0 copy.100
  283.1 0.0 copy-done.1
  (22 shorter events, 0.2 us)
Async XLA Ops:
  0.0 23.3 %copy-start = (f32[128,512]{1,0:T(8,128)S(1)}, f32[128,512]{1,0:T(8,128)}, u32[]{:S(2)}) copy-start(f32[128,512]{1,0:T(8,128)} %param.12) | copy-start | bytes 786436
  5.9 4.0 %copy-start.4 = (f32[2,4,128,512]{3,2,1,0:T(8,128)S(1)}, f32[2,4,128,512]{3,2,1,0:T(8,128)}, u32[]{:S(2)}) copy-start(f32[2,4,128,512]{3,2,1,0:T(8,128)} %param.10) | copy-start | bytes 6291460
  13.9 9.4 %copy-start.5 = (f32[128,512]{1,0:T(8,128)S(1)}, f32[128,512]{1,0:T(8,128)}, u32[]{:S(2)}) copy-start(f32[128,512]{1,0:T(8,128)} %param.11) | copy-start | bytes 786436
  13.9 105.4 %all-to-all-start = ((f32[4,4,128,512]{3,1,0,2:T(4,128)}), f32[4,4,128,512]{3,1,0,2:T(4,128)}, u32[]{:S(2)}, u32[]{:S(2)}) async-start(f32[4,4,128,512]{3,1,0,2:T(4,128)} %pad_maximum_fusion), calls=%async_computation | async-start | bytes 8388608 | tf_op jit(solution)/shard_map/all_to_all | solution.py:160
  197.7 19.9 %all-to-all-start.2 = ((f32[8,16,512]{2,1,0:T(8,128)}), f32[8,16,512]{2,1,0:T(8,128)S(1)}, u32[]{:S(2)}, u32[]{:S(2)}) async-start(f32[8,16,512]{2,1,0:T(8,128)} %stack.33), calls=%async_computation.2 | async-start | bytes 524288 | tf_op jit(solution)/shard_map/all_to_all | solution.py:183
  217.6 58.2 %all-to-all-start.1 = ((f32[2,32,16,512]{3,2,0,1:T(8,128)}), f32[2,32,16,512]{3,2,0,1:T(8,128)S(1)}, u32[]{:S(2)}, u32[]{:S(2)}) async-start(f32[2,32,16,512]{3,2,0,1:T(8,128)} %copy.92), calls=%async_computation.1 | async-start | bytes 4194304 | tf_op jit(solution)/shard_map/all_to_all | solution.py:181
  225.9 6.5 %collective-permute-start = (f32[5,4,1,512]{3,2,1,0:T(1,128)S(1)}, f32[5,4,1,512]{3,2,1,0:T(1,128)S(1)}, u32[]{:S(2)}, u32[]{:S(2)}) collective-permute-start(f32[5,4,1,512]{3,2,1,0:T(1,128)S(1)} %get-tuple-element.49), channel_id=1, source_target_pairs={{0,4},{4,8},{8,12},{12,16},{16,20},{20,24},{24,28},{28,0},{1,5},{5... | collective-permute-start | bytes 122888 | tf_op jit(solution)/shard_map/ppermute | solution.py:21
  229.1 5.7 %collective-permute-start.1 = (f32[5,4,1,512]{3,2,1,0:T(1,128)S(1)}, f32[5,4,1,512]{3,2,1,0:T(1,128)S(1)}, u32[]{:S(2)}, u32[]{:S(2)}) collective-permute-start(f32[5,4,1,512]{3,2,1,0:T(1,128)S(1)} %get-tuple-element.50), channel_id=1, source_target_pairs={{4,0},{8,4},{12,8},{16,12},{20,16},{24,20},{28,24},{0,28},{5,1},{9... | collective-permute-start | bytes 122888 | tf_op jit(solution)/shard_map/ppermute | solution.py:24
  241.2 4.4 %collective-permute-start.2 = (f32[5,4,130,1]{2,0,3,1:T(8,128)S(1)}, f32[5,4,130,1]{2,0,3,1:T(8,128)S(1)}, u32[]{:S(2)}, u32[]{:S(2)}) collective-permute-start(f32[5,4,130,1]{2,0,3,1:T(8,128)S(1)} %copy.83), channel_id=1, source_target_pairs={{0,1},{1,2},{2,3},{3,0},{4,5},{5,6},{6,7},{7,4},{8,9},{9,10},{10,1... | collective-permute-start | bytes 31208 | tf_op jit(solution)/shard_map/ppermute | solution.py:21
  243.8 3.4 %collective-permute-start.3 = (f32[5,4,130,1]{2,0,3,1:T(8,128)S(1)}, f32[5,4,130,1]{2,0,3,1:T(8,128)S(1)}, u32[]{:S(2)}, u32[]{:S(2)}) collective-permute-start(f32[5,4,130,1]{2,0,3,1:T(8,128)S(1)} %copy.84), channel_id=1, source_target_pairs={{1,0},{2,1},{3,2},{0,3},{5,4},{6,5},{7,6},{4,7},{9,8},{10,9},{11,1... | collective-permute-start | bytes 31208 | tf_op jit(solution)/shard_map/ppermute | solution.py:24
  275.8 1.2 copy-start.2
  275.8 1.5 copy-start.3
  280.8 2.3 copy-start.1
